TPU v7x, 128 devices: a whole 4x4x4 slice. The times are simulated.
128 devices in a mesh: row: 8 (over z, core), col: 16 (over y, x).
Axes of the slice: x: 4, y: 4, z: 4, core: 2. Of those that a mesh axis runs over, the one named last changes fastest.
Arguments:
- hidden: bfloat16 [1408, 16384], P('col', 'row'), may hold values from -18 to 18
- gain_in: bfloat16 [1408], replicated, may hold values from 0.5 to 1.5
- w_query: bfloat16 [1408, 1408], P('col'), may hold values from -0.3125 to 0.3125
- w_pair: bfloat16 [2, 1408, 1408], P(None, 'col'), may hold values from -0.15625 to 0.15625
- kv_cache: bfloat16 [2, 1408, 16384], P(None, 'col', 'row'), may hold values from -103 to 103
- recompute_rows: int32 [8, 200], P('row'), may hold values from 0 to 2047, as said below
- segment_ids: int32 [16384], P('row'), may hold values from -1 to 1, as said below
- w_out: bfloat16 [1408, 1408], P('col'), may hold values from -0.3125 to 0.3125
- gain_merge: bfloat16 [1408], replicated, may hold values from 0.5 to 1.5
- w_merge: bfloat16 [4, 1408, 1408], P(None, 'col'), may hold values from -0.078125 to 0.078125
- requests: int32 [8, 16, 85], P('row'), may hold values from -1 to 511, as said below
Outputs:
- delivered: bfloat16 [8, 16, 85, 1408], P('row', 'col')
Inputs may be any that keep to these rules, and one draw needn't show every extreme that they name: `segment_ids`: ids do not fall along the tokens except to -1 for the padding at the end; every image covers a multiple of 4 tokens and starts at a multiple of 4. `recompute_rows`: the 200 offsets of one index of row are distinct. `requests`: for each index of row, the lists of all owners together name each of its 512 merged tokens exactly once; unused slots hold -1 and follow the used ones.
All inputs are finite; a program needn't handle non-finite values.
Results may differ from a plain program's by a relative error of at most 0.025.
The roundings to bfloat16 on the way count: a program that leaves them out, or rounds other values in their place, can miss the bound.
Values may be sent and summed in bfloat16 or wider, within the bound.
A program may use at most 128 MiB of HBM per device.

v0:
```python
import jax
import jax.numpy as jnp
from jax import lax
from jax.sharding import PartitionSpec as P

HD = 88
EPSILON = 1e-06
MASKED = -1e30
KEY_BLOCK = 1024


def on_device(
    hidden,
    gain_in,
    w_query,
    w_pair,
    kv_cache,
    recompute_rows,
    segment_ids,
    w_out,
    gain_merge,
    w_merge,
    requests,
):
    local_width, tok_rows = hidden.shape
    model_width = w_query.shape[1]
    heads_here = local_width // HD
    score_scale = HD ** (-0.5)
    column_start = lax.axis_index("col") * local_width
    full_rows = lax.all_gather(hidden, "col", axis=0, tiled=True)
    full_float = full_rows.astype(jnp.float32)
    in_mean = jnp.sum(full_float, axis=0, keepdims=True) / model_width
    in_square = jnp.sum(full_float * full_float, axis=0, keepdims=True) / model_width
    normed = (
        (full_float - in_mean)
        * lax.rsqrt(in_square - in_mean * in_mean + EPSILON)
        * gain_in.astype(jnp.float32)[:, None]
    ).astype(jnp.bfloat16)
    queries = jnp.dot(w_query, normed, preferred_element_type=jnp.float32).astype(jnp.bfloat16)
    picked_rows = recompute_rows[0]
    normed_picked = jnp.take(normed, picked_rows, axis=1)
    fresh_pairs = jnp.dot(
        w_pair.reshape(2 * local_width, model_width),
        normed_picked,
        preferred_element_type=jnp.float32,
    )
    fresh_pairs = fresh_pairs.astype(jnp.bfloat16).reshape(2, local_width, -1)
    keys_values = kv_cache.at[:, :, picked_rows].set(fresh_pairs)
    query_heads = queries.reshape(heads_here, HD, tok_rows)
    segment_grid = segment_ids.reshape(1, 1, tok_rows)

    def take_block(carried, pair_block, segment_block):
        running_max, running_sum, weighted = carried
        key_block = pair_block[0].reshape(heads_here, HD, -1)
        value_block = pair_block[1].reshape(heads_here, HD, -1)
        scores = (
            jnp.einsum("hdq,hdk->hqk", query_heads, key_block, preferred_element_type=jnp.float32)
            * score_scale
        )
        allowed = (segment_ids[:, None] == segment_block[None, :])[None, :, :]
        new_max = jnp.maximum(running_max, jnp.max(jnp.where(allowed, scores, MASKED), axis=2))
        weights_exp = jnp.where(allowed, jnp.exp(scores - new_max[:, :, None]), 0.0)
        factor = jnp.exp(running_max - new_max)
        running_sum = running_sum * factor + jnp.sum(weights_exp, axis=2)
        product = jnp.einsum(
            "hqk,hdk->hdq",
            weights_exp.astype(jnp.bfloat16),
            value_block,
            preferred_element_type=jnp.float32,
        )
        weighted = weighted * factor[:, None, :] + product
        return (new_max, running_sum, weighted)

    starting = (
        jnp.full((heads_here, tok_rows), MASKED, jnp.float32),
        jnp.zeros((heads_here, tok_rows), jnp.float32),
        jnp.zeros((heads_here, HD, tok_rows), jnp.float32),
    )
    carried = starting
    pair_rows = lax.all_gather(keys_values, "row", axis=2, tiled=True)
    segment_rows = lax.all_gather(segment_grid, "row", axis=2, tiled=True)
    segment_line = segment_rows[0, 0]
    piece_rows = pair_rows.shape[2]
    whole_blocks = piece_rows // KEY_BLOCK

    def loop_body(block_index, loop_state):
        pair_block = lax.dynamic_slice_in_dim(pair_rows, block_index * KEY_BLOCK, KEY_BLOCK, 2)
        segment_block = lax.dynamic_slice_in_dim(
            segment_line, block_index * KEY_BLOCK, KEY_BLOCK, 0
        )
        return take_block(loop_state, pair_block, segment_block)

    carried = lax.fori_loop(0, whole_blocks, loop_body, carried)
    running_max, running_sum, weighted = carried
    attended = (
        (weighted / running_sum[:, None, :]).astype(jnp.bfloat16).reshape(local_width, tok_rows)
    )
    gain_part = lax.dynamic_slice_in_dim(gain_merge, column_start, local_width, 0).astype(
        jnp.float32
    )[:, None]
    partial_out = lax.dot_general(
        w_out, attended, (((0,), (0,)), ((), ())), preferred_element_type=jnp.float32
    )
    summed = lax.psum(partial_out.astype(jnp.bfloat16), "col").astype(jnp.float32)
    updated = full_float + summed
    row_mean = jnp.sum(updated, axis=0, keepdims=True) / model_width
    row_square = jnp.sum(updated * updated, axis=0, keepdims=True) / model_width
    own_part = lax.dynamic_slice_in_dim(updated, column_start, local_width, 0)
    merger_in = (
        (own_part - row_mean) * lax.rsqrt(row_square - row_mean * row_mean + EPSILON) * gain_part
    ).astype(jnp.bfloat16)
    merged_rows = tok_rows // 4
    grouped = merger_in.reshape(local_width, merged_rows, 4)
    merged = jnp.einsum("cgi,icd->gd", grouped, w_merge, preferred_element_type=jnp.float32)
    wanted_rows = requests[0]
    is_valid = wanted_rows >= 0
    safe_index = jnp.where(is_valid, wanted_rows, 0)
    picked = jnp.where(is_valid[:, :, None], merged[safe_index], 0.0)
    owned_rows = lax.psum_scatter(
        picked.astype(jnp.bfloat16), "col", scatter_dimension=0, tiled=True
    )
    return owned_rows.reshape(1, 1, owned_rows.shape[1], model_width)


def solution(mesh):
    placed = (
        P("col", "row"),
        P(),
        P("col", None),
        P(None, "col", None),
        P(None, "col", "row"),
        P("row", None),
        P("row"),
        P("col", None),
        P(),
        P(None, "col", None),
        P("row", None, None),
    )
    return jax.shard_map(
        on_device,
        mesh=mesh,
        in_specs=placed,
        out_specs=P("row", "col", None, None),
        check_vma=False,
    )
```

profile of v0, /device:TPU:0, one launch (start us, length us, event | category | flops | bytes accessed | tf_op | source)
XLA Modules:
  0.0 632.6 jit_solution(8836994563244462151)
XLA Ops:
  11.8 59.0 %all-gather.4.cloned.1.call-done = bf16[1408,2048]{1,0:T(8,128)(2,1)} async-done(((bf16[88,2048]{1,0:T(8,128)(2,1)}), bf16[1408,2048]{1,0:T(8,128)(2,1)}) %all-gather.4.cloned.1.call-update) | async-done | bytes 5767184 | tf_op jit(solution)/shard_map/all_gather | solution.py:30
  70.7 8.4 %copy.22 = bf16[1408,2048]{0,1:T(8,128)(2,1)} copy(bf16[1408,2048]{1,0:T(8,128)(2,1)} %all-gather.4.cloned.1.call-done) | data formatting | bytes 11534336 | tf_op jit(solution)/shard_map/all_gather | solution.py:30
  93.2 6.9 %scatter_fusion = bf16[2,88,2048]{1,0,2:T(2,128)(2,1)S(1)} fusion(bf16[2,88,2048]{1,0,2:T(2,128)(2,1)S(1)} %copy.24, s32[200]{0:T(256)S(1)} %bitcast.104, bf16[200,2,88]{2,1,0:T(2,128)(2,1)S(1)} %bitcast.99), kind=kCustom, calls=%fused_computation.2 | custom fusion | bytes 212000 | tf_op jit(solution)/shard_map/scatter | solution.py:48
  102.1 13.4 %all-gather = s32[16384]{0:T(1024)S(1)} all-gather(s32[2048]{0:T(1024)S(1)} %copy-done.2), channel_id=2, replica_groups=mesh['row'=8,'col'=16] {'row'}, dimensions={0}, use_global_device_ids=true | all-gather | bytes 73728 | tf_op jit(solution)/shard_map/all_gather | solution.py:81
  120.2 20.6 %all-gather.6.cloned.1.call-done = bf16[2,88,16384]{2,1,0:T(8,128)(2,1)} async-done(((bf16[2,88,2048]{2,1,0:T(8,128)(2,1)}), bf16[2,88,16384]{2,1,0:T(8,128)(2,1)}) %all-gather.6.cloned.1.call-update) | async-done | bytes 5767184 | tf_op jit(solution)/shard_map/all_gather | solution.py:80
  140.9 249.8 %while.18 = (s32[]{:T(128)}, f32[1,2048]{1,0:T(1,128)S(1)}, f32[1,2048]{1,0:T(1,128)S(1)}, f32[1,88,2048]{2,1,0:T(8,128)S(1)}, s32[2048]{0:T(1024)S(1)}, /*index...) while((s32[]{:T(128)}, f32[1,2048]{1,0:T(1,128)S(1)}, ...), condition=%wide.region_6.7_spmd.clone, body=%wide.region_3.0_spmd.clone.sunk | while | flops 768108544 | bytes 27504848 | solution.py:93
  140.9 5.6 fusion.46
  156.5 5.5 fusion.46
  166.7 5.4 fusion.50
  172.1 5.5 fusion.46
  187.7 5.5 fusion.46
  197.9 5.4 fusion.50
  203.4 5.5 fusion.46
  219.0 5.5 fusion.46
  229.1 5.4 fusion.50
  234.6 5.5 fusion.46
  250.2 5.5 fusion.46
  260.4 5.4 fusion.50
  265.8 5.5 fusion.46
  281.4 5.5 fusion.46
  291.6 5.4 fusion.50
  297.0 5.5 fusion.46
  312.6 5.5 fusion.46
  322.8 5.4 fusion.50
  328.3 5.5 fusion.46
  343.9 5.5 fusion.46
  359.5 5.5 fusion.46
  375.1 5.5 fusion.46
  396.1 116.2 %all-reduce.3.cloned.1.call-done = bf16[1408,2048]{0,1:T(8,128)(2,1)} async-done(((bf16[1408,2048]{0,1:T(8,128)(2,1)}), bf16[1408,2048]{0,1:T(8,128)(2,1)}) %all-reduce.3.cloned.1.call-update) | async-done | bytes 5767184 | tf_op jit(solution)/shard_map/psum | solution.py:104
  512.3 10.2 %fusion.33 = (f32[2048]{0:T(1024)S(1)}, f32[2048]{0:T(1024)S(1)}, f32[1408,2048]{0,1:T(8,128)}) fusion(bf16[1408,2048]{0,1:T(8,128)(2,1)} %all-reduce.3.cloned.1.call-done, bf16[1408,2048]{0,1:T(8,128)(2,1)} %copy.22), kind=kLoop, calls=%fused_computation.65 | loop fusion | flops 17297408 | bytes 23085056 | tf_op jit(solution)/shard_map/reduce_sum | solution.py:106
  526.0 6.0 gather_fusion.1
  539.8 86.3 %reduce-scatter.4.cloned.1.call-done = bf16[1,85,1408]{2,1,0:T(8,128)(2,1)} async-done(((bf16[16,85,1408]{2,1,0:T(8,128)(2,1)}), bf16[1,85,1408]{2,1,0:T(8,128)(2,1)}) %reduce-scatter.4.cloned.1.call-update) | async-done | bytes 239376
  (139 shorter events, 170.8 us)
Async XLA Ops:
  6.5 518.4 %copy-start = (bf16[4,88,1408]{2,1,0:T(8,128)(2,1)S(1)}, bf16[4,88,1408]{2,1,0:T(8,128)(2,1)}, u32[]{:S(2)}) copy-start(bf16[4,88,1408]{2,1,0:T(8,128)(2,1)} %param.22) | copy-start | bytes 2973700
  6.5 64.2 %all-gather.4.cloned.1.call-start = ((), (), s32[]{:S(2)}) async-start(), calls=%async_computation.1 | async-start | bytes 6127616 | tf_op jit(solution)/shard_map/all_gather | solution.py:30
  7.3 133.6 %all-gather.6.cloned.1.call-start = ((), (), s32[]{:S(2)}) async-start(), calls=%async_computation.2 | async-start | bytes 6488064 | tf_op jit(solution)/shard_map/all_gather | solution.py:80
  79.1 4.5 copy-start.1
  83.6 9.0 %copy-start.6 = (bf16[2,88,1408]{2,1,0:T(8,128)(2,1)S(1)}, bf16[2,88,1408]{2,1,0:T(8,128)(2,1)}, u32[]{:S(2)}) copy-start(bf16[2,88,1408]{2,1,0:T(8,128)(2,1)} %param.16) | copy-start | bytes 1486852
  87.6 14.5 %copy-start.2 = (s32[2048]{0:T(1024)S(1)}, s32[2048]{0:T(1024)}, u32[]{:S(2)}) copy-start(s32[2048]{0:T(1024)} %param.19) | copy-start | bytes 24580
  87.6 27.9 %copy-start.3 = (bf16[88,1408]{1,0:T(8,128)(2,1)S(1)}, bf16[88,1408]{1,0:T(8,128)(2,1)}, u32[]{:S(2)}) copy-start(bf16[88,1408]{1,0:T(8,128)(2,1)} %param.15) | copy-start | bytes 743428
  102.1 410.2 %all-reduce.3.cloned.1.call-start = ((), (), s32[]{:S(2)}) async-start(), calls=%async_computation.3 | async-start | bytes 11534336 | tf_op jit(solution)/shard_map/psum | solution.py:104
  140.9 249.8 %copy-start.4 = (bf16[88,1408]{1,0:T(8,128)(2,1)S(1)}, bf16[88,1408]{1,0:T(8,128)(2,1)}, u32[]{:S(2)}) copy-start(bf16[88,1408]{1,0:T(8,128)(2,1)} %param.20) | copy-start | bytes 743428
  390.7 4.5 copy-start.5
  395.0 231.1 %reduce-scatter.4.cloned.1.call-start = ((), (), s32[]{:S(2)}) async-start(), calls=%async_computation.4 | async-start | bytes 4212736
Sparse Core Ops, SparseCore 0:
  9.5 61.1 all-gather.3
  102.2 38.6 all-gather.5
  395.1 117.1 all-reduce.2
  539.9 86.1 reduce-scatter.3
where the time goes:
time: 634 us; the launch traced here: 633 us
  waiting for transfers between devices  283 us (45%)
  matrix products  185 us (29%)
  other arithmetic  102 us (16%)
  local copies, waits for them, and re-layouts  35 us (6%)
  blocking collectives  13.4 us (2%)
  between operations  13.3 us (2%)
    psum x1, waiting for transfers between devices, on_device(): lax.psum(partial_out.astype(jnp.bfloat16), 'col').astype(jnp.float32)  116 us
    dot_general x16, matrix products, take_block(): jnp.einsum('hdq,hdk->hqk', query_heads, key_block, preferred_element_type...  88.5 us
    unnamed x5, waiting for transfers between devices  87 us
    dot_general x16, matrix products, take_block(): jnp.einsum('hqk,hdk->hdq', weights_exp.astype(jnp.bfloat16), value_block,...  86.2 us
    reduce_sum x16, other arithmetic, take_block(): running_sum = running_sum * factor + jnp.sum(weights_exp, axis=2)  73.2 us
    all_gather x1, waiting for transfers between devices, on_device(): full_rows = lax.all_gather(hidden, 'col', axis=0, tiled=True)  59 us
    all_gather x1, waiting for transfers between devices, on_device(): pair_rows = lax.all_gather(keys_values, 'row', axis=2, tiled=True)  20.6 us
    all_gather x1, blocking collectives, on_device(): segment_rows = lax.all_gather(segment_grid, 'row', axis=2, tiled=True)  13.4 us
  transfers between devices with their start and end apart: 4, of which 4 were waited for; matrix products, arithmetic and copies ran while one was open for 2% of the time, Pallas kernels for 0%

commit v1 on v0

--- a/solution.py
+++ b/solution.py
@@ -77,7 +77,9 @@
         jnp.zeros((heads_here, HD, tok_rows), jnp.float32),
     )
     carried = starting
-    pair_rows = lax.all_gather(keys_values, "row", axis=2, tiled=True)
+    pair_rows = jnp.concatenate(
+        lax.all_to_all(jnp.stack([keys_values] * lax.axis_size("row")), "row", 0, 0), axis=2
+    )
     segment_rows = lax.all_gather(segment_grid, "row", axis=2, tiled=True)
     segment_line = segment_rows[0, 0]
     piece_rows = pair_rows.shape[2]

time: 634 us -> 684 us (1.079)
  blocking collectives: 13.4 us -> 72.2 us
  waiting for transfers between devices: 283 us -> 261 us
  local copies, waits for them, and re-layouts: 35 us -> 43 us
    all_gather x1, blocking collectives: 13.4 us -> 72.2 us  [on_device(): segment_rows = lax.all_gather(segment_grid, 'row', axis=2, tiled=True)]
    all_gather x1 -> x0, waiting for transfers between devices: 20.6 us -> none  [on_device(): pair_rows = lax.all_gather(keys_values, 'row', axis=2, tiled=True)]
    unnamed x5 -> x4, waiting for transfers between devices: 87 us -> 87 us
  transfers between devices with their start and end apart: 4 -> 4, of which waited for: 4 -> 3; matrix products, arithmetic and copies ran while one was open for 2% -> 1% of each run, Pallas kernels for 0% -> 0%
where the time goes in v1:
time: 684 us; the launch traced here: 683 us
  waiting for transfers between devices  261 us (38%)
  matrix products  185 us (27%)
  other arithmetic  102 us (15%)
  blocking collectives  72.2 us (11%)
  local copies, waits for them, and re-layouts  43 us (6%)
  between operations  13.3 us (2%)
    psum x1, waiting for transfers between devices, on_device(): lax.psum(partial_out.astype(jnp.bfloat16), 'col').astype(jnp.float32)  115 us
    dot_general x16, matrix products, take_block(): jnp.einsum('hdq,hdk->hqk', query_heads, key_block, preferred_element_type...  88.6 us
    unnamed x4, waiting for transfers between devices  87 us
    dot_general x16, matrix products, take_block(): jnp.einsum('hqk,hdk->hdq', weights_exp.astype(jnp.bfloat16), value_block,...  86.4 us
    reduce_sum x16, other arithmetic, take_block(): running_sum = running_sum * factor + jnp.sum(weights_exp, axis=2)  73.2 us
    all_gather x1, blocking collectives, on_device(): segment_rows = lax.all_gather(segment_grid, 'row', axis=2, tiled=True)  72.2 us
    all_gather x1, waiting for transfers between devices, on_device(): full_rows = lax.all_gather(hidden, 'col', axis=0, tiled=True)  59 us
  transfers between devices with their start and end apart: 4, of which 3 were waited for; matrix products, arithmetic and copies ran while one was open for 1% of the time, Pallas kernels for 0%

profile of v1, /device:TPU:0, one launch (start us, length us, event | category | flops | bytes accessed | tf_op | source)
XLA Modules:
  0.0 682.6 jit_solution(6239626202895411671)
XLA Ops:
  11.7 59.0 %all-gather.3.cloned.1.call-done = bf16[1408,2048]{1,0:T(8,128)(2,1)} async-done(((bf16[88,2048]{1,0:T(8,128)(2,1)}), bf16[1408,2048]{1,0:T(8,128)(2,1)}) %all-gather.3.cloned.1.call-update) | async-done | bytes 5767184 | tf_op jit(solution)/shard_map/all_gather | solution.py:30
  70.7 8.4 %copy.27 = bf16[1408,2048]{0,1:T(8,128)(2,1)} copy(bf16[1408,2048]{1,0:T(8,128)(2,1)} %all-gather.3.cloned.1.call-done) | data formatting | bytes 11534336 | tf_op jit(solution)/shard_map/all_gather | solution.py:30
  93.1 6.9 %scatter_fusion = bf16[2,88,2048]{1,0,2:T(2,128)(2,1)S(1)} fusion(bf16[2,88,2048]{1,0,2:T(2,128)(2,1)S(1)} %copy.29, s32[200]{0:T(256)S(1)} %bitcast.108, bf16[200,2,88]{2,1,0:T(2,128)(2,1)S(1)} %bitcast.103), kind=kCustom, calls=%fused_computation.2 | custom fusion | bytes 212000 | tf_op jit(solution)/shard_map/scatter | solution.py:48
  108.8 72.2 %all-gather = s32[16384]{0:T(1024)S(1)} all-gather(s32[2048]{0:T(1024)S(1)} %copy-done.2), channel_id=2, replica_groups=mesh['row'=8,'col'=16] {'row'}, dimensions={0}, use_global_device_ids=true | all-gather | bytes 73728 | tf_op jit(solution)/shard_map/all_gather | solution.py:83
  185.7 6.1 copy.33
  191.8 250.1 %while.18 = (s32[]{:T(128)}, f32[1,2048]{1,0:T(1,128)S(1)}, f32[1,2048]{1,0:T(1,128)S(1)}, f32[1,88,2048]{2,1,0:T(8,128)S(1)}, s32[2048]{0:T(1024)S(1)}, /*index...) while((s32[]{:T(128)}, f32[1,2048]{1,0:T(1,128)S(1)}, ...), condition=%wide.region_6.7_spmd.clone, body=%wide.region_3.0_spmd.clone.sunk | while | flops 768108544 | bytes 27504848 | solution.py:95
  191.8 5.6 fusion.46
  202.1 5.4 fusion.50
  207.5 5.5 fusion.46
  223.1 5.5 fusion.46
  233.3 5.4 fusion.50
  238.8 5.5 fusion.46
  254.4 5.5 fusion.46
  270.0 5.5 fusion.46
  285.7 5.5 fusion.46
  295.8 5.4 fusion.50
  301.3 5.5 fusion.46
  316.9 5.5 fusion.46
  332.6 5.5 fusion.46
  348.2 5.5 fusion.46
  358.4 5.4 fusion.50
  363.8 5.5 fusion.46
  379.5 5.5 fusion.46
  389.6 5.4 fusion.50
  395.1 5.5 fusion.46
  410.7 5.5 fusion.46
  420.9 5.4 fusion.50
  426.4 5.5 fusion.46
  447.4 114.9 %all-reduce.3.cloned.1.call-done = bf16[1408,2048]{0,1:T(8,128)(2,1)} async-done(((bf16[1408,2048]{0,1:T(8,128)(2,1)}), bf16[1408,2048]{0,1:T(8,128)(2,1)}) %all-reduce.3.cloned.1.call-update) | async-done | bytes 5767184 | tf_op jit(solution)/shard_map/psum | solution.py:106
  562.3 10.2 %fusion.33 = (f32[2048]{0:T(1024)S(1)}, f32[2048]{0:T(1024)S(1)}, f32[1408,2048]{0,1:T(8,128)}) fusion(bf16[1408,2048]{0,1:T(8,128)(2,1)} %all-reduce.3.cloned.1.call-done, bf16[1408,2048]{0,1:T(8,128)(2,1)} %copy.27), kind=kLoop, calls=%fused_computation.65 | loop fusion | flops 17297408 | bytes 23085056 | tf_op jit(solution)/shard_map/reduce_sum | solution.py:108
  576.0 6.0 gather_fusion.1
  589.8 86.2 %reduce-scatter.4.cloned.1.call-done = bf16[1,85,1408]{2,1,0:T(8,128)(2,1)} async-done(((bf16[16,85,1408]{2,1,0:T(8,128)(2,1)}), bf16[1,85,1408]{2,1,0:T(8,128)(2,1)}) %reduce-scatter.4.cloned.1.call-update) | async-done | bytes 239376
  (140 shorter events, 177.5 us)
Async XLA Ops:
  6.5 568.4 %copy-start = (bf16[4,88,1408]{2,1,0:T(8,128)(2,1)S(1)}, bf16[4,88,1408]{2,1,0:T(8,128)(2,1)}, u32[]{:S(2)}) copy-start(bf16[4,88,1408]{2,1,0:T(8,128)(2,1)} %param.22) | copy-start | bytes 2973700
  6.5 64.2 %all-gather.3.cloned.1.call-start = ((), (), s32[]{:S(2)}) async-start(), calls=%async_computation.2 | async-start | bytes 6127616 | tf_op jit(solution)/shard_map/all_gather | solution.py:30
  79.1 4.5 copy-start.1
  83.6 9.0 %copy-start.6 = (bf16[2,88,1408]{2,1,0:T(8,128)(2,1)S(1)}, bf16[2,88,1408]{2,1,0:T(8,128)(2,1)}, u32[]{:S(2)}) copy-start(bf16[2,88,1408]{2,1,0:T(8,128)(2,1)} %param.16) | copy-start | bytes 1486852
  100.8 8.0 %copy-start.2 = (s32[2048]{0:T(1024)S(1)}, s32[2048]{0:T(1024)}, u32[]{:S(2)}) copy-start(s32[2048]{0:T(1024)} %param.19) | copy-start | bytes 24580
  100.8 80.3 %copy-start.3 = (bf16[88,1408]{1,0:T(8,128)(2,1)S(1)}, bf16[88,1408]{1,0:T(8,128)(2,1)}, u32[]{:S(2)}) copy-start(bf16[88,1408]{1,0:T(8,128)(2,1)} %param.15) | copy-start | bytes 743428
  104.0 81.7 %all-to-all-start = ((bf16[8,2,88,2048]{3,2,1,0:T(8,128)(2,1)}), bf16[8,2,88,2048]{3,2,1,0:T(8,128)(2,1)}, u32[]{:S(2)}, u32[]{:S(2)}) async-start(bf16[8,2,88,2048]{3,2,1,0:T(8,128)(2,1)} %stack.2), calls=%async_computation | async-start | bytes 11534336 | tf_op jit(solution)/shard_map/all_to_all | solution.py:81
  108.7 453.6 %all-reduce.3.cloned.1.call-start = ((), (), s32[]{:S(2)}) async-start(), calls=%async_computation.3 | async-start | bytes 11534336 | tf_op jit(solution)/shard_map/psum | solution.py:106
  191.8 250.1 %copy-start.4 = (bf16[88,1408]{1,0:T(8,128)(2,1)S(1)}, bf16[88,1408]{1,0:T(8,128)(2,1)}, u32[]{:S(2)}) copy-start(bf16[88,1408]{1,0:T(8,128)(2,1)} %param.20) | copy-start | bytes 743428
  442.0 4.5 copy-start.5
  446.2 229.8 %reduce-scatter.4.cloned.1.call-start = ((), (), s32[]{:S(2)}) async-start(), calls=%async_computation.4 | async-start | bytes 4212736
Sparse Core Ops, SparseCore 0:
  9.5 61.1 all-gather.2
  446.3 115.9 all-reduce.2
  589.9 86.0 reduce-scatter.3
